TPU v7x, 128 devices: a whole 4x4x4 slice. The times are simulated.
128 devices in a mesh: group: 4 (over x), bulk: 32 (over z, y, core).
Axes of the slice: x: 4, y: 4, z: 4, core: 2. Of those that a mesh axis runs over, the one named last changes fastest.
Arguments:
- rhs: float32 [512, 64, 128], P(('group', 'bulk')), may hold values from -90 to 90, as said below
- diag_tiles: float32 [512, 128, 128], P(('group', 'bulk')), may hold values from -0.06 to 0.06
- offdiag_blocks: float32 [512, 11, 128, 128], P(('group', 'bulk')), may hold values from -0.026 to 0.026
- coupling: float32 [256, 4, 128, 128], P(('group', 'bulk')), may hold values from -0.05 to 0.05, as said below
- col_index: int32 [512, 11], replicated, may hold values from 0 to 511, as said below
- load: int32 [512], replicated, may hold values from 3 to 11
- new_slot: int32 [512], replicated, may hold values from 0 to 511, as said below
Outputs:
- solution_out: float32 [512, 64, 128], P(('group', 'bulk'))
- residual_out: float32 [512, 64, 128], P(('group', 'bulk'))
Inputs may be any that keep to these rules, and one draw needn't show every extreme that they name: `rhs`: made of random entries times scales of the rows and of the columns. `coupling`: entry [d * 2 + k, h] is the transpose of entry [(h * 32 + d % 32) * 2 + k, d // 32]. `col_index`: for each part g and each tile position t, the column t of the 128 block rows of part g is a permutation of that part's slots g * 128 to (g + 1) * 128 - 1. Of the 44 entries of the 4 block rows of one device (slots d * 4 to (d + 1) * 4 - 1), at most 2 name slots of any one device, and exactly 2 name slots of some device. `new_slot`: A permutation. On every device exactly one block row moves, from a slot k with 2 <= k % 4; it stays in its part, goes from owner b to owner b XOR m, where m (1 to 31) is one number for the whole part, and takes the slot that the moving row of that device leaves.
All inputs are finite; a program needn't handle non-finite values.
Results may differ from a plain program's by a relative error of at most 0.0003.
Values sent between devices are 32-bit elements; how exact they have to be, the bound alone decides.
A program may use at most 64 MiB of HBM per device.

v0:
```python
import jax
import jax.numpy as jnp
from jax import lax
from jax.sharding import PartitionSpec as P

highest = lax.Precision.HIGHEST
diagonal_shift = 4.0


def chol_apply(matrix, right):
    factor = jnp.linalg.cholesky(matrix)
    middle = lax.linalg.triangular_solve(factor, right, left_side=True, lower=True)
    return lax.linalg.triangular_solve(factor, middle, left_side=True, lower=True, transpose_a=True)


def gram(left, right):
    return jnp.einsum("snt,smt->nm", left, right, precision=highest)


def sym(m):
    return 0.5 * (m + m.T)


def mm(a, b):
    return jnp.dot(a, b, precision=highest)


def off_part(vectors, diag, masked, column_ids, coupling):
    boundary_rows = coupling.shape[0]
    part_count = coupling.shape[1]
    border = lax.all_gather(vectors[:boundary_rows], "group", axis=0, tiled=True)
    own = jnp.einsum("rnj,rij->rni", vectors, diag, precision=highest)
    returned = jnp.einsum("rni,rkij->rknj", vectors, masked, precision=highest)
    panel = lax.all_gather(vectors, "bulk", axis=0, tiled=True)
    picked = panel[column_ids]
    own = own + jnp.einsum("rknj,rkij->rni", picked, masked, precision=highest)
    border = border.reshape((part_count, boundary_rows) + vectors.shape[1:])
    crossed = jnp.einsum("khij,hknj->kni", coupling, border, precision=highest)
    return (own.at[:boundary_rows].add(crossed), returned.reshape((-1,) + vectors.shape[1:]), panel)


def coefficients(n0, n1, n2, n3):
    n = n0.shape[0]
    eye = jnp.eye(n, dtype=n0.dtype)
    n0, n1, n2, n3 = (sym(n0), sym(n1), sym(n2), sym(n3))
    delta = chol_apply(diagonal_shift * n0 + n1, n1)
    alpha = (eye - delta) / diagonal_shift
    b = -alpha
    cross = mm(delta.T, mm(n1, b))
    gram_new = sym(mm(delta.T, mm(n0, delta)) + cross + cross.T + mm(b.T, mm(n2, b)))
    beta = chol_apply(n0, gram_new)
    a = delta + beta
    c1 = mm(a.T, mm(n1, b))
    c2 = mm(a.T, mm(n2, b))
    pp = mm(a.T, mm(n0, a)) + c1 + c1.T + mm(b.T, mm(n2, b))
    pep = mm(a.T, mm(n1, a)) + c2 + c2.T + mm(b.T, mm(n3, b))
    alpha2 = chol_apply(sym(diagonal_shift * pp + pep), gram_new)
    ba = mm(b, alpha2)
    aa = mm(a, alpha2)
    sol = (alpha + aa, ba)
    res = (delta - diagonal_shift * aa, b - diagonal_shift * ba - aa, -ba)
    return (sol, res)


def local(rhs, diag_tiles, offdiag_blocks, coupling, col_index, load, new_slot):
    row_count = rhs.shape[0]
    off_count = offdiag_blocks.shape[1]
    bulk_count = lax.axis_size("bulk")
    group_rows = row_count * bulk_count
    group_base = lax.axis_index("group") * group_rows
    first = lax.axis_index("bulk") * row_count
    cols = lax.dynamic_slice_in_dim(col_index, group_base, group_rows) - group_base
    moved = lax.dynamic_slice_in_dim(new_slot, group_base, group_rows) - group_base
    loads = lax.dynamic_slice_in_dim(load, group_base + first, row_count)
    my_cols = lax.dynamic_slice_in_dim(cols, first, row_count)
    my_new = lax.dynamic_slice_in_dim(moved, first, row_count)
    tile_ids = jnp.arange(off_count, dtype=jnp.int32)
    mask = (tile_ids[None, :] < loads[:, None]).astype(jnp.float32)
    masked = offdiag_blocks * mask[:, :, None, None]
    u0 = rhs
    own, returned, panel0 = off_part(u0, diag_tiles, masked, my_cols, coupling)
    buffer = jax.ops.segment_sum(returned, my_cols.reshape(-1), num_segments=group_rows)
    u1 = own + lax.psum_scatter(buffer, "bulk", scatter_dimension=0, tiled=True)
    own, returned, panel1 = off_part(u1, diag_tiles, masked, my_cols, coupling)
    ids = jnp.concatenate([moved[my_cols.reshape(-1)], my_new])
    buffer = jax.ops.segment_sum(jnp.concatenate([returned, own]), ids, num_segments=group_rows)
    u2 = lax.psum_scatter(buffer, "bulk", scatter_dimension=0, tiled=True)
    inverse = jnp.zeros_like(moved).at[moved].set(jnp.arange(group_rows, dtype=jnp.int32))
    mine = lax.dynamic_slice_in_dim(inverse, first, row_count)
    v0, v1 = (panel0[mine], panel1[mine])
    grams = jnp.stack([gram(v0, v0), gram(v0, v1), gram(v1, v1), gram(v1, u2)])
    grams = lax.psum(grams, ("group", "bulk"))
    sol, res = coefficients(grams[0], grams[1], grams[2], grams[3])
    basis = jnp.concatenate([v0, v1, u2], axis=1)
    zero = jnp.zeros_like(sol[0])
    weights = jnp.concatenate(
        [jnp.concatenate(sol + (zero,), axis=0), jnp.concatenate(res, axis=0)], axis=1
    )
    out = jnp.einsum("mn,smt->snt", weights, basis, precision=highest)
    n = rhs.shape[1]
    return (out[:, :n], out[:, n:])


def solution(mesh):
    return jax.shard_map(
        local,
        mesh=mesh,
        in_specs=(
            P(("group", "bulk"), None, None),
            P(("group", "bulk"), None, None),
            P(("group", "bulk"), None, None, None),
            P(("group", "bulk"), None, None, None),
            P(),
            P(),
            P(),
        ),
        out_specs=(P(("group", "bulk"), None, None), P(("group", "bulk"), None, None)),
        check_vma=False,
    )
```

profile of v0, /device:TPU:1, one launch (start us, length us, event | category | flops | bytes accessed | tf_op | source)
XLA Modules:
  0.0 494.6 jit_solution(10182201475086260046)
XLA Ops:
  9.8 3.8 fusion.4
  13.5 2.5 broadcast.140.clone
  16.0 6.9 %scatter_fusion = f32[128,64,128]{2,1,0:T(8,128)} fusion(f32[128,64,128]{2,1,0:T(8,128)} %broadcast.140.clone, s32[44]{0:T(128)S(1)} %reshape.206, f32[44,64,128]{2,1,0:T(8,128)S(1)} %bitcast.248), kind=kCustom, calls=%fused_computation.6 | custom fusion | flops 360448 | bytes 4325552 | tf_op jit(solution)/shard_map/scatter-add | solution.py:82
  25.9 12.7 %all_gather.13 = f32[8,64,128]{2,1,0:T(8,128)} all-gather(f32[2,64,128]{2,1,0:T(8,128)} %slice.81), channel_id=1, replica_groups=mesh['group'=4,'bulk'=32] {'group'}, dimensions={0}, use_global_device_ids=true | all-gather | bytes 327680 | tf_op jit(solution)/shard_map/all_gather | solution.py:31
  38.5 21.5 %all-gather.3.cloned.1.call-done = f32[128,64,128]{2,1,0:T(8,128)} async-done(((f32[4,64,128]{2,1,0:T(8,128)}), f32[128,64,128]{2,1,0:T(8,128)}) %all-gather.3.cloned.1.call-update) | async-done | bytes 4194320 | tf_op jit(solution)/shard_map/all_gather | solution.py:34
  60.1 4.0 gather_fusion.1
  64.1 4.8 fusion.12
  68.9 1.3 convolution_add_fusion.1
  70.2 2.1 fusion.21
  72.4 71.0 %reduce-scatter.3.cloned.1.call-done = f32[4,64,128]{2,1,0:T(8,128)} async-done(((f32[128,64,128]{2,1,0:T(8,128)}), f32[4,64,128]{2,1,0:T(8,128)}) %reduce-scatter.3.cloned.1.call-update) | async-done | bytes 131088 | tf_op jit(solution)/shard_map/reduce_scatter | solution.py:83
  143.4 1.6 add.181
  147.7 10.6 %all_gather.15 = f32[8,64,128]{2,1,0:T(8,128)} all-gather(f32[2,64,128]{2,1,0:T(8,128)S(1)} %slice.102), channel_id=1, replica_groups=mesh['group'=4,'bulk'=32] {'group'}, dimensions={0}, use_global_device_ids=true | all-gather | bytes 327680 | tf_op jit(solution)/shard_map/all_gather | solution.py:31
  158.3 4.1 fusion.2
  162.4 31.4 %all-gather.5.cloned.1.call-done = f32[128,64,128]{2,1,0:T(8,128)} async-done(((f32[4,64,128]{2,1,0:T(8,128)}), f32[128,64,128]{2,1,0:T(8,128)}) %all-gather.5.cloned.1.call-update) | async-done | bytes 4194320 | tf_op jit(solution)/shard_map/all_gather | solution.py:34
  193.8 3.9 gather_fusion.4
  197.7 4.9 fusion.15
  204.1 2.5 broadcast.140
  206.6 6.9 %scatter_fusion.1 = f32[128,64,128]{2,1,0:T(8,128)} fusion(f32[128,64,128]{2,1,0:T(8,128)} %broadcast.140, s32[48]{0:T(128)S(1)} %pad_add_fusion, f32[48,64,128]{2,1,0:T(8,128)S(1)} %pad_maximum_fusion), kind=kCustom, calls=%fused_computation.7 | custom fusion | flops 393216 | bytes 4718784 | tf_op jit(solution)/shard_map/scatter-add | solution.py:86
  213.6 1.2 scatter_custom_fusion
  214.9 2.7 gather_fusion
  217.9 2.7 gather_fusion.2
  221.1 72.2 %reduce-scatter.5.cloned.1.call-done = f32[4,64,128]{2,1,0:T(8,128)} async-done(((f32[128,64,128]{2,1,0:T(8,128)}), f32[4,64,128]{2,1,0:T(8,128)}) %reduce-scatter.5.cloned.1.call-update) | async-done | bytes 131088 | tf_op jit(solution)/shard_map/reduce_scatter | solution.py:87
  293.4 1.2 convolution_bitcast_fusion.3
  295.2 146.3 %all-reduce.2.cloned.1.call-done = f32[4,64,64]{2,1,0:T(8,128)} async-done(((f32[4,64,64]{2,1,0:T(8,128)}), f32[4,64,64]{2,1,0:T(8,128)}) %all-reduce.2.cloned.1.call-update) | async-done | bytes 65552 | tf_op jit(solution)/shard_map/psum | solution.py:92
  443.6 5.9 %cholesky.59 = f32[64,64]{1,0:T(8,128)S(1)} custom-call(f32[64,64]{1,0:T(8,128)S(1)} %copy.82), custom_call_target="Cholesky" | custom-call | tf_op jit(solution)/shard_map/jit(cholesky)/cholesky | solution.py:11
  450.8 4.9 custom-call.13
  456.7 5.9 %cholesky.70 = f32[64,64]{1,0:T(8,128)S(1)} custom-call(f32[64,64]{1,0:T(8,128)S(1)} %copy.85), custom_call_target="Cholesky" | custom-call | tf_op jit(solution)/shard_map/jit(cholesky)/cholesky | solution.py:11
  463.9 4.9 custom-call.15
  468.8 1.0 fusion.67
  471.9 1.0 fusion.45
  473.9 5.8 %cholesky.81 = f32[64,64]{1,0:T(8,128)S(1)} custom-call(f32[64,64]{1,0:T(8,128)S(1)} %fusion.51), custom_call_target="Cholesky" | custom-call | tf_op jit(solution)/shard_map/jit(cholesky)/cholesky | solution.py:11
  481.1 4.9 custom-call.17
  (112 shorter events, 23.2 us)
Async XLA Ops:
  7.2 63.1 %copy-start = (f32[2,4,128,128]{3,2,1,0:T(8,128)S(1)}, f32[2,4,128,128]{3,2,1,0:T(8,128)}, u32[]{:S(2)}) copy-start(f32[2,4,128,128]{3,2,1,0:T(8,128)} %param.19) | copy-start | bytes 1572868
  7.2 52.9 %all-gather.3.cloned.1.call-start = ((), (), s32[]{:S(2)}) async-start(), calls=%async_computation.2 | async-start | bytes 4325376 | tf_op jit(solution)/shard_map/all_gather | solution.py:34
  7.9 135.5 %reduce-scatter.3.cloned.1.call-start = ((), (), s32[]{:S(2)}) async-start(), calls=%async_computation.3 | async-start | bytes 4325376 | tf_op jit(solution)/shard_map/reduce_scatter | solution.py:83
  22.9 0.9 copy-start.4
  22.9 41.2 %copy-start.1 = (f32[4,11,128,128]{3,2,1,0:T(8,128)S(1)}, f32[4,11,128,128]{3,2,1,0:T(8,128)}, u32[]{:S(2)}) copy-start(f32[4,11,128,128]{3,2,1,0:T(8,128)} %param.18) | copy-start | bytes 8650756
  22.9 170.9 %all-gather.5.cloned.1.call-start = ((), (), s32[]{:S(2)}) async-start(), calls=%async_computation.4 | async-start | bytes 4325376 | tf_op jit(solution)/shard_map/all_gather | solution.py:34
  64.1 4.8 copy-start.7
  64.1 6.1 %copy-start.6 = (f32[8,64,128]{2,1,0:T(8,128)S(1)}, f32[8,64,128]{2,1,0:T(8,128)}, u32[]{:S(2)}) copy-start(f32[8,64,128]{2,1,0:T(8,128)} %all_gather.13) | copy-start | bytes 786436
  145.0 148.3 %reduce-scatter.5.cloned.1.call-start = ((), (), s32[]{:S(2)}) async-start(), calls=%async_computation.5 | async-start | bytes 4325376 | tf_op jit(solution)/shard_map/reduce_scatter | solution.py:87
  197.7 4.9 copy-start.3
  197.7 4.9 %copy-start.8 = (f32[4,128,128]{2,1,0:T(8,128)S(1)}, f32[4,128,128]{2,1,0:T(8,128)}, u32[]{:S(2)}) copy-start(f32[4,128,128]{2,1,0:T(8,128)} %param.17) | copy-start | bytes 786436
  197.7 5.6 %copy-start.5 = (f32[8,64,128]{2,1,0:T(8,128)S(1)}, f32[8,64,128]{2,1,0:T(8,128)}, u32[]{:S(2)}) copy-start(f32[8,64,128]{2,1,0:T(8,128)} %all_gather.15) | copy-start | bytes 786436
  197.7 6.2 %copy-start.2 = (f32[4,11,128,64]{2,3,1,0:T(8,128)S(1)}, f32[4,11,128,64]{2,3,1,0:T(8,128)}, u32[]{:S(2)}) copy-start(f32[4,11,128,64]{2,3,1,0:T(8,128)} %fusion.2) | copy-start | bytes 4325380
  213.5 228.1 %all-reduce.2.cloned.1.call-start = ((), (), s32[]{:S(2)}) async-start(), calls=%async_computation.6 | async-start | bytes 262144 | tf_op jit(solution)/shard_map/psum | solution.py:92
  294.5 192.4 %copy-start.9 = (f32[4,64,128]{2,1,0:T(8,128)S(1)}, f32[4,64,128]{2,1,0:T(8,128)}, u32[]{:S(2)}) copy-start(f32[4,64,128]{2,1,0:T(8,128)} %reduce-scatter.5.cloned.1.call-done) | copy-start | bytes 393220
Sparse Core Ops, SparseCore 0:
  10.2 49.7 all-gather.2
  63.7 79.6 reduce-scatter.2
  146.2 47.5 all-gather.4
  213.6 79.7 reduce-scatter.4
  298.5 142.9 all-reduce.1
where the time goes:
time: 496 us; the launch traced here: 495 us
  waiting for transfers between devices  343 us (69%)
  other arithmetic  55.1 us (11%)
  matrix products  30.5 us (6%)
  local copies, waits for them, and re-layouts  28.1 us (6%)
  blocking collectives  23.2 us (5%)
  between operations  14.3 us (3%)
    psum x1, waiting for transfers between devices, local(): grams = lax.psum(grams, ('group', 'bulk'))  146 us
    reduce_scatter x1, waiting for transfers between devices, local(): u2 = lax.psum_scatter(buffer, 'bulk', scatter_dimension=0, tiled=True)  72.2 us
    reduce_scatter x1, waiting for transfers between devices, local(): u1 = own + lax.psum_scatter(buffer, 'bulk', scatter_dimension=0, tiled=True)  71 us
    all_gather x2, waiting for transfers between devices, off_part(): panel = lax.all_gather(vectors, 'bulk', axis=0, tiled=True)  52.9 us
    all_gather x2, blocking collectives, off_part(): lax.all_gather(vectors[:boundary_rows], 'group', axis=0, tiled=True)  23.2 us
    another operation x9, other arithmetic, chol_apply(): factor = jnp.linalg.cholesky(matrix)  19.6 us
    another operation x6, other arithmetic, chol_apply(): lax.linalg.triangular_solve(factor, middle, left_side=True, lower=True, t...  16.6 us
  transfers between devices with their start and end apart: 5, of which 5 were waited for; matrix products, arithmetic and copies ran while one was open for 9% of the time, Pallas kernels for 0%

commit v1 on v0

--- a/solution.py
+++ b/solution.py
@@ -5,6 +5,11 @@
 
 highest = lax.Precision.HIGHEST
 diagonal_shift = 4.0
+
+
+def add_all(x, name):
+    blocks = lax.all_gather(x, name)
+    return jnp.sum(blocks, axis=0)
 
 
 def chol_apply(matrix, right):
@@ -89,7 +94,7 @@
     mine = lax.dynamic_slice_in_dim(inverse, first, row_count)
     v0, v1 = (panel0[mine], panel1[mine])
     grams = jnp.stack([gram(v0, v0), gram(v0, v1), gram(v1, v1), gram(v1, u2)])
-    grams = lax.psum(grams, ("group", "bulk"))
+    grams = add_all(grams, ("group", "bulk"))
     sol, res = coefficients(grams[0], grams[1], grams[2], grams[3])
     basis = jnp.concatenate([v0, v1, u2], axis=1)
     zero = jnp.zeros_like(sol[0])

time: 496 us -> 437 us (0.88)
  waiting for transfers between devices: 343 us -> 280 us
  other arithmetic: 55.1 us -> 61.8 us
    psum x1 -> x0, waiting for transfers between devices: 146 us -> none  [local(): grams = lax.psum(grams, ('group', 'bulk'))]
    all_gather x0 -> x1, waiting for transfers between devices: none -> 83 us  [add_all(): blocks = lax.all_gather(x, name)]
    reduce_sum x0 -> x1, other arithmetic: none -> 7.53 us  [add_all(): return jnp.sum(blocks, axis=0)]
  transfers between devices with their start and end apart: 5 -> 5, of which waited for: 5 -> 5; matrix products, arithmetic and copies ran while one was open for 9% -> 10% of each run, Pallas kernels for 0% -> 0%
where the time goes in v1:
time: 437 us; the launch traced here: 436 us
  waiting for transfers between devices  280 us (64%)
  other arithmetic  61.8 us (14%)
  matrix products  29 us (7%)
  local copies, waits for them, and re-layouts  27.3 us (6%)
  blocking collectives  23.2 us (5%)
  between operations  14.3 us (3%)
    all_gather x1, waiting for transfers between devices, add_all(): blocks = lax.all_gather(x, name)  83 us
    reduce_scatter x1, waiting for transfers between devices, local(): u2 = lax.psum_scatter(buffer, 'bulk', scatter_dimension=0, tiled=True)  72.2 us
    reduce_scatter x1, waiting for transfers between devices, local(): u1 = own + lax.psum_scatter(buffer, 'bulk', scatter_dimension=0, tiled=True)  71 us
    all_gather x2, waiting for transfers between devices, off_part(): panel = lax.all_gather(vectors, 'bulk', axis=0, tiled=True)  52.9 us
    all_gather x2, blocking collectives, off_part(): lax.all_gather(vectors[:boundary_rows], 'group', axis=0, tiled=True)  23.2 us
    another operation x9, other arithmetic, chol_apply(): factor = jnp.linalg.cholesky(matrix)  19.6 us
    another operation x6, other arithmetic, chol_apply(): lax.linalg.triangular_solve(factor, middle, left_side=True, lower=True, t...  16.6 us
    dot_general x2, matrix products, off_part(): own = own + jnp.einsum('rknj,rkij->rni', picked, masked, precision=highest)  9.75 us
  transfers between devices with their start and end apart: 5, of which 5 were waited for; matrix products, arithmetic and copies ran while one was open for 10% of the time, Pallas kernels for 0%

profile of v1, /device:TPU:1, one launch (start us, length us, event | category | flops | bytes accessed | tf_op | source)
XLA Modules:
  0.0 435.8 jit_solution(12975206923112830053)
XLA Ops:
  9.8 3.8 fusion.4
  13.5 2.5 broadcast.140.clone
  16.0 6.9 %scatter_fusion = f32[128,64,128]{2,1,0:T(8,128)} fusion(f32[128,64,128]{2,1,0:T(8,128)} %broadcast.140.clone, s32[44]{0:T(128)S(1)} %reshape.206, f32[44,64,128]{2,1,0:T(8,128)S(1)} %bitcast.250), kind=kCustom, calls=%fused_computation.6 | custom fusion | flops 360448 | bytes 4325552 | tf_op jit(solution)/shard_map/scatter-add | solution.py:87
  25.9 12.7 %all_gather.19 = f32[8,64,128]{2,1,0:T(8,128)} all-gather(f32[2,64,128]{2,1,0:T(8,128)} %slice.81), channel_id=1, replica_groups=mesh['group'=4,'bulk'=32] {'group'}, dimensions={0}, use_global_device_ids=true | all-gather | bytes 327680 | tf_op jit(solution)/shard_map/all_gather | solution.py:36
  38.5 21.5 %all-gather.5.cloned.1.call-done = f32[128,64,128]{2,1,0:T(8,128)} async-done(((f32[4,64,128]{2,1,0:T(8,128)}), f32[128,64,128]{2,1,0:T(8,128)}) %all-gather.5.cloned.1.call-update) | async-done | bytes 4194320 | tf_op jit(solution)/shard_map/all_gather | solution.py:39
  60.1 4.0 gather_fusion.1
  64.1 4.8 %fusion.12 = f32[4,64,128]{2,1,0:T(8,128)S(1)} fusion(f32[4,11,64,128]{3,2,1,0:T(8,128)} %bitcast.252, f32[4,11,128,128]{3,2,1,0:T(8,128)S(1)} %copy-done.1, f32[4,11]{1,0:T(4,128)S(1)} %fusion.85), kind=kOutput, calls=%fused_computation.22 | convolution fusion | flops 554369024 | bytes 4456624 | tf_op jit(solution)/shard_map/rknj,rkij->rni/dot_general | solution.py:41
  68.9 1.3 convolution_add_fusion.1
  70.2 2.1 fusion.21
  72.4 71.0 %reduce-scatter.3.cloned.1.call-done = f32[4,64,128]{2,1,0:T(8,128)} async-done(((f32[128,64,128]{2,1,0:T(8,128)}), f32[4,64,128]{2,1,0:T(8,128)}) %reduce-scatter.3.cloned.1.call-update) | async-done | bytes 131088 | tf_op jit(solution)/shard_map/reduce_scatter | solution.py:88
  143.4 1.6 add.179
  146.9 0.8 slice.102
  147.7 10.6 %all_gather.21 = f32[8,64,128]{2,1,0:T(8,128)} all-gather(f32[2,64,128]{2,1,0:T(8,128)S(1)} %slice.102), channel_id=1, replica_groups=mesh['group'=4,'bulk'=32] {'group'}, dimensions={0}, use_global_device_ids=true | all-gather | bytes 327680 | tf_op jit(solution)/shard_map/all_gather | solution.py:36
  158.3 4.1 fusion.2
  162.4 31.4 %all-gather.7.cloned.1.call-done = f32[128,64,128]{2,1,0:T(8,128)} async-done(((f32[4,64,128]{2,1,0:T(8,128)}), f32[128,64,128]{2,1,0:T(8,128)}) %all-gather.7.cloned.1.call-update) | async-done | bytes 4194320 | tf_op jit(solution)/shard_map/all_gather | solution.py:39
  193.8 3.9 gather_fusion.4
  197.7 4.9 %fusion.15 = f32[4,64,128]{2,1,0:T(8,128)S(1)} fusion(f32[4,11,64,128]{3,2,1,0:T(8,128)} %bitcast.251, f32[4,11,128,128]{3,2,1,0:T(8,128)S(1)} %copy-done.1, f32[4,11]{1,0:T(4,128)S(1)} %fusion.85), kind=kOutput, calls=%fused_computation.23 | convolution fusion | flops 554369024 | bytes 4456624 | tf_op jit(solution)/shard_map/rknj,rkij->rni/dot_general | solution.py:41
  204.1 2.5 broadcast.140
  206.6 6.9 %scatter_fusion.1 = f32[128,64,128]{2,1,0:T(8,128)} fusion(f32[128,64,128]{2,1,0:T(8,128)} %broadcast.140, s32[48]{0:T(128)S(1)} %pad_add_fusion, f32[48,64,128]{2,1,0:T(8,128)S(1)} %pad_maximum_fusion), kind=kCustom, calls=%fused_computation.7 | custom fusion | flops 393216 | bytes 4718784 | tf_op jit(solution)/shard_map/scatter-add | solution.py:91
  213.6 1.2 scatter_custom_fusion
  214.9 2.7 gather_fusion
  217.9 2.7 gather_fusion.2
  221.1 72.2 %reduce-scatter.5.cloned.1.call-done = f32[4,64,128]{2,1,0:T(8,128)} async-done(((f32[128,64,128]{2,1,0:T(8,128)}), f32[4,64,128]{2,1,0:T(8,128)}) %reduce-scatter.5.cloned.1.call-update) | async-done | bytes 131088 | tf_op jit(solution)/shard_map/reduce_scatter | solution.py:92
  293.4 1.2 convolution_bitcast_fusion.3
  295.2 83.0 %all-gather.9.cloned.1.call-done = f32[512,64,64]{2,1,0:T(8,128)} async-done(((f32[4,64,64]{2,1,0:T(8,128)}), f32[512,64,64]{2,1,0:T(8,128)}) %all-gather.9.cloned.1.call-update) | async-done | bytes 8388624 | tf_op jit(solution)/shard_map/all_gather | solution.py:11
  378.3 7.5 %reduce_sum.9 = f32[4,64,64]{2,1,0:T(8,128)S(1)} reduce(f32[128,4,64,64]{3,2,1,0:T(8,128)} %bitcast.248, f32[]{:T(128)} %constant.110.clone.1), dimensions={0}, to_apply=%region_5.0 | reduce | flops 2080768 | bytes 8454148 | tf_op jit(solution)/shard_map/reduce_sum | solution.py:12
  386.3 5.9 %cholesky.59 = f32[64,64]{1,0:T(8,128)S(1)} custom-call(f32[64,64]{1,0:T(8,128)S(1)} %copy.82), custom_call_target="Cholesky" | custom-call | tf_op jit(solution)/shard_map/jit(cholesky)/cholesky | solution.py:16
  393.5 4.9 %custom-call.13 = f32[1,64,64]{1,2,0:T(8,128)S(1)} custom-call(f32[1,64,64]{2,1,0:T(8,128)S(1)} %fusion.41), custom_call_target="InvertDiagBlocksLowerTriangular" | custom-call | tf_op jit(solution)/shard_map/triangular_solve/custom-call.2 | solution.py:18
  399.4 5.9 %cholesky.70 = f32[64,64]{1,0:T(8,128)S(1)} custom-call(f32[64,64]{1,0:T(8,128)S(1)} %copy.85), custom_call_target="Cholesky" | custom-call | tf_op jit(solution)/shard_map/jit(cholesky)/cholesky | solution.py:16
  406.6 4.9 %custom-call.15 = f32[1,64,64]{1,2,0:T(8,128)S(1)} custom-call(f32[1,64,64]{2,1,0:T(8,128)S(1)} %fusion.42), custom_call_target="InvertDiagBlocksLowerTriangular" | custom-call | tf_op jit(solution)/shard_map/triangular_solve/custom-call.2 | solution.py:18
  415.1 5.8 %cholesky.81 = f32[64,64]{1,0:T(8,128)S(1)} custom-call(f32[64,64]{1,0:T(8,128)S(1)} %fusion.51), custom_call_target="Cholesky" | custom-call | tf_op jit(solution)/shard_map/jit(cholesky)/cholesky | solution.py:16
  422.3 4.9 %custom-call.17 = f32[1,64,64]{1,2,0:T(8,128)S(1)} custom-call(f32[1,64,64]{2,1,0:T(8,128)S(1)} %fusion.43), custom_call_target="InvertDiagBlocksLowerTriangular" | custom-call | tf_op jit(solution)/shard_map/triangular_solve/custom-call.2 | solution.py:18
  (113 shorter events, 21.2 us)
Async XLA Ops:
  7.2 63.1 %copy-start = (f32[2,4,128,128]{3,2,1,0:T(8,128)S(1)}, f32[2,4,128,128]{3,2,1,0:T(8,128)}, u32[]{:S(2)}) copy-start(f32[2,4,128,128]{3,2,1,0:T(8,128)} %param.19) | copy-start | bytes 1572868
  7.2 52.9 %all-gather.5.cloned.1.call-start = ((), (), s32[]{:S(2)}) async-start(), calls=%async_computation.2 | async-start | bytes 4325376 | tf_op jit(solution)/shard_map/all_gather | solution.py:39
  7.9 135.5 %reduce-scatter.3.cloned.1.call-start = ((), (), s32[]{:S(2)}) async-start(), calls=%async_computation.3 | async-start | bytes 4325376 | tf_op jit(solution)/shard_map/reduce_scatter | solution.py:88
  22.9 0.9 copy-start.4
  22.9 41.2 %copy-start.1 = (f32[4,11,128,128]{3,2,1,0:T(8,128)S(1)}, f32[4,11,128,128]{3,2,1,0:T(8,128)}, u32[]{:S(2)}) copy-start(f32[4,11,128,128]{3,2,1,0:T(8,128)} %param.18) | copy-start | bytes 8650756
  22.9 170.9 %all-gather.7.cloned.1.call-start = ((), (), s32[]{:S(2)}) async-start(), calls=%async_computation.4 | async-start | bytes 4325376 | tf_op jit(solution)/shard_map/all_gather | solution.py:39
  64.1 4.8 %copy-start.7 = (f32[4,128,128]{2,1,0:T(8,128)S(1)}, f32[4,128,128]{2,1,0:T(8,128)}, u32[]{:S(2)}) copy-start(f32[4,128,128]{2,1,0:T(8,128)} %param.17) | copy-start | bytes 786436
  64.1 6.1 %copy-start.6 = (f32[8,64,128]{2,1,0:T(8,128)S(1)}, f32[8,64,128]{2,1,0:T(8,128)}, u32[]{:S(2)}) copy-start(f32[8,64,128]{2,1,0:T(8,128)} %all_gather.19) | copy-start | bytes 786436
  145.0 148.3 %reduce-scatter.5.cloned.1.call-start = ((), (), s32[]{:S(2)}) async-start(), calls=%async_computation.5 | async-start | bytes 4325376 | tf_op jit(solution)/shard_map/reduce_scatter | solution.py:92
  197.7 4.9 %copy-start.3 = (f32[4,64,128]{2,1,0:T(8,128)S(1)}, f32[4,64,128]{2,1,0:T(8,128)}, u32[]{:S(2)}) copy-start(f32[4,64,128]{2,1,0:T(8,128)} %add.179) | copy-start | bytes 393220
  197.7 4.9 %copy-start.8 = (f32[4,128,128]{2,1,0:T(8,128)S(1)}, f32[4,128,128]{2,1,0:T(8,128)}, u32[]{:S(2)}) copy-start(f32[4,128,128]{2,1,0:T(8,128)} %param.17) | copy-start | bytes 786436
  197.7 5.6 %copy-start.5 = (f32[8,64,128]{2,1,0:T(8,128)S(1)}, f32[8,64,128]{2,1,0:T(8,128)}, u32[]{:S(2)}) copy-start(f32[8,64,128]{2,1,0:T(8,128)} %all_gather.21) | copy-start | bytes 786436
  197.7 6.2 %copy-start.2 = (f32[4,11,128,64]{2,3,1,0:T(8,128)S(1)}, f32[4,11,128,64]{2,3,1,0:T(8,128)}, u32[]{:S(2)}) copy-start(f32[4,11,128,64]{2,3,1,0:T(8,128)} %fusion.2) | copy-start | bytes 4325380
  213.5 164.8 %all-gather.9.cloned.1.call-start = ((), (), s32[]{:S(2)}) async-start(), calls=%async_computation.6 | async-start | bytes 16908288 | tf_op jit(solution)/shard_map/all_gather | solution.py:11
  385.8 42.3 %copy-start.9 = (f32[4,64,128]{2,1,0:T(8,128)S(1)}, f32[4,64,128]{2,1,0:T(8,128)}, u32[]{:S(2)}) copy-start(f32[4,64,128]{2,1,0:T(8,128)} %reduce-scatter.5.cloned.1.call-done) | copy-start | bytes 393220
Sparse Core Ops, SparseCore 0:
  10.2 49.7 all-gather.4
  63.7 79.6 reduce-scatter.2
  146.2 47.5 all-gather.6
  213.6 79.7 reduce-scatter.4
  296.9 81.2 all-gather.8
